TPU v7x, 32 devices: a whole 2x2x4 slice. The times are simulated.
32 devices in a mesh: band: 4 (over x, core), grid: 8 (over z, y).
Axes of the slice: x: 2, y: 2, z: 4, core: 2. Of those that a mesh axis runs over, the one named last changes fastest.
Arguments:
- orbitals: bfloat16 [16384, 2048], P('grid', 'band'), may hold values from -6 to 6
- projectors: bfloat16 [64, 8, 128], replicated, may hold values from -0.5 to 0.5
- sphere_start: int32 [64], replicated, may hold values from 0 to 1920, as said below
- proj_count: int32 [64], replicated, may hold values from 1 to 8
- owner_slab: int32 [64], replicated, may hold values from 0 to 7, as said below
- correlation_coef: float32 [64, 8, 8], replicated, as said below
Outputs:
- rotated: bfloat16 [16384, 2048], P(('grid', 'band'))
Inputs may be any that keep to these rules, and one draw needn't show every extreme that they name: `sphere_start`: a multiple of 128. `owner_slab`: every slab owns exactly 8 atoms. `correlation_coef`: each atom's matrix is symmetric positive definite.
All inputs are finite; a program needn't handle non-finite values.
Results may differ from a plain program's by a relative error of at most 0.0049.
Values may be sent and summed in bfloat16 or wider, within the bound.
A program may use at most 128 MiB of HBM per device.

v0:
```python
import jax
import jax.numpy as jnp
from jax import lax
from jax.sharding import PartitionSpec as P

SPH = 128
NPMAX = 8
A_SLAB = 8


def inverse_factor(matrix):
    order = matrix.shape[0]
    if order <= 512 or order % 2 != 0:
        lower = jnp.linalg.cholesky(matrix)
        identity = jnp.eye(order, dtype=matrix.dtype)
        return lax.linalg.triangular_solve(lower, identity, left_side=True, lower=True)
    half = order // 2
    upper_inv = inverse_factor(matrix[:half, :half])
    below = jnp.dot(matrix[half:, :half], upper_inv.T, precision=lax.Precision.HIGHEST)
    schur = matrix[half:, half:] - jnp.dot(below, below.T, precision=lax.Precision.HIGHEST)
    lower_inv = inverse_factor(schur)
    corner = -jnp.dot(
        lower_inv,
        jnp.dot(below, upper_inv, precision=lax.Precision.HIGHEST),
        precision=lax.Precision.HIGHEST,
    )
    top = jnp.concatenate([upper_inv, jnp.zeros((half, order - half), matrix.dtype)], axis=1)
    bottom = jnp.concatenate([corner, lower_inv], axis=1)
    return jnp.concatenate([top, bottom], axis=0)


def slab_atoms(owner_slab, slab):
    atoms = owner_slab.shape[0]
    keyed = jnp.where(owner_slab == slab, 0, 1) * atoms + jnp.arange(atoms, dtype=jnp.int32)
    return jnp.argsort(keyed, stable=True)[:A_SLAB]


def atom_terms(source, weights, starts, counts, coefs, valid):

    def take_rows(offset):
        return lax.dynamic_slice_in_dim(source, offset, SPH, 0)

    sphere_rows = jax.vmap(take_rows)(starts)
    correlations = jnp.einsum(
        "aij,ajn->ain", weights, sphere_rows, preferred_element_type=jnp.float32
    )
    active = (jnp.arange(NPMAX)[None, :] < counts[:, None]) & valid[:, None]
    correlations = jnp.where(active[:, :, None], correlations, jnp.zeros_like(correlations))
    weighted = jnp.einsum("aij,ajn->ain", coefs, correlations, precision=lax.Precision.HIGHEST)
    return (correlations, weighted)


def shards(orbitals, projectors, sphere_start, proj_count, owner_slab, correlation_coef):
    band_index = lax.axis_index("band")
    slab = lax.axis_index("grid")
    total_rows = orbitals.shape[0] * lax.axis_size("grid")
    chosen = slab_atoms(owner_slab, slab)
    weights = projectors[chosen]
    counts = proj_count[chosen]
    coefs = correlation_coef[chosen]
    mine = lax.all_to_all(orbitals, "band", split_axis=0, concat_axis=1, tiled=True)
    height = mine.shape[0]
    width_all = mine.shape[1]
    gram = jnp.dot(mine.T, mine, preferred_element_type=jnp.float32) * (1.0 / total_rows)
    offsets = sphere_start[chosen] - band_index * height
    valid = (offsets >= 0) & (offsets < height)
    offsets = jnp.clip(offsets, 0, height - SPH)
    correlations, weighted = atom_terms(mine, weights, offsets, counts, coefs, valid)
    paw = jnp.dot(
        weighted.reshape(-1, width_all).T,
        correlations.reshape(-1, width_all),
        precision=lax.Precision.HIGHEST,
    )
    metric = lax.psum(gram + paw, ("band", "grid"))
    inverse = inverse_factor(metric).astype(jnp.bfloat16)
    return jnp.dot(mine, inverse.T, preferred_element_type=jnp.float32).astype(jnp.bfloat16)


def solution(mesh):
    in_specs = (P("grid", "band"), P(), P(), P(), P(), P())
    out_specs = P(("grid", "band"), None)
    return jax.shard_map(shards, mesh=mesh, in_specs=in_specs, out_specs=out_specs, check_vma=False)
```

profile of v0, /device:TPU:0, one launch (start us, length us, event | category | flops | bytes accessed | tf_op | source)
XLA Modules:
  0.0 1109.8 jit_solution(1387231611529632680)
XLA Ops:
  16.0 21.5 %all-to-all-done = bf16[4,512,512]{2,1,0:T(8,128)(2,1)} async-done(((bf16[4,512,512]{2,1,0:T(8,128)(2,1)}), bf16[4,512,512]{2,1,0:T(8,128)(2,1)}, u32[]{:S(2)}, u32[]{:S(2)}) %all-to-all-start) | async-done | bytes 2097184 | tf_op jit(solution)/shard_map/all_to_all | solution.py:61
  40.3 20.2 %while.9 = (s32[]{:T(128)}, bf16[512,2048]{0,1:T(8,128)(2,1)S(1)}, s32[8,2]{0,1:T(2,128)S(1)}, bf16[8,128,2048]{2,1,0:T(8,128)(2,1)}, s32[]{:T(128)}) while((s32[]{:T(128)}, bf16[512,2048]{0,1:T(8,128)(2,1)S(1)}, s32[8,2]{0,1:T(2,128)S(1)}, bf16[8,128,2048]{2,1,0:T(8,128)(2,1)}, s32[]{:T(128)}) %tuple.122), condition=%wide.while_cond.1, body=%wide.while_body.1.sunk | while | flops 2 | bytes 3146333 | solution.py:41
  64.7 14.1 %fusion.178 = f32[2048,2048,1]{0,1,2:T(8,128)S(1)} fusion(f32[8,8,2048]{2,1,0:T(8,128)S(1)} %fusion.177, f32[8,8,2048]{2,1,0:T(8,128)S(1)} %convolution_select_fusion), kind=kOutput, calls=%fused_computation.329 | convolution fusion | flops 3221225472 | bytes 17825792 | tf_op jit(solution)/shard_map/dot_general | solution.py:69
  78.8 12.9 %bitcast_add_fusion = f32[2048,2048]{0,1:T(8,128)} fusion(f32[2048,2048,1]{0,1,2:T(8,128)S(1)} %fusion.178, bf16[512,2048]{0,1:T(8,128)(2,1)} %copy-done.4), kind=kOutput, calls=%fused_computation.16 | convolution fusion | flops 4303355904 | bytes 35651584 | tf_op jit(solution)/shard_map/dot_general | solution.py:64
  91.9 279.4 %all-reduce.7.cloned.1.call-done = f32[2048,2048]{0,1:T(8,128)} async-done(((f32[2048,2048]{0,1:T(8,128)}), f32[2048,2048]{0,1:T(8,128)}) %all-reduce.7.cloned.1.call-update) | async-done | bytes 16777232 | tf_op jit(solution)/shard_map/psum | solution.py:74
  374.4 11.7 %cholesky.462 = f32[128,128]{1,0:T(8,128)S(1)} custom-call(f32[128,128]{1,0:T(8,128)S(1)} %cholesky.746), custom_call_target="Cholesky" | custom-call | tf_op jit(solution)/shard_map/jit(cholesky)/cholesky | solution.py:14
  396.9 11.7 %cholesky.481 = f32[128,128]{1,0:T(8,128)S(1)} custom-call(f32[128,128]{1,0:T(8,128)S(1)} %cholesky.750), custom_call_target="Cholesky" | custom-call | tf_op jit(solution)/shard_map/jit(cholesky)/cholesky | solution.py:14
  419.1 11.9 %cholesky.502 = f32[128,128]{1,0:T(8,128)S(1)} custom-call(f32[128,128]{1,0:T(8,128)S(1)} %cholesky.755), custom_call_target="Cholesky" | custom-call | tf_op jit(solution)/shard_map/jit(cholesky)/cholesky | solution.py:14
  442.1 11.7 %cholesky.519 = f32[128,128]{1,0:T(8,128)S(1)} custom-call(f32[128,128]{1,0:T(8,128)S(1)} %convolution_subtract_fusion.25), custom_call_target="Cholesky" | custom-call | tf_op jit(solution)/shard_map/jit(cholesky)/cholesky | solution.py:14
  466.0 39.7 %custom-call.38 = f32[4,128,128]{1,2,0:T(8,128)S(1)} custom-call(f32[4,128,128]{2,1,0:T(8,128)S(1)} %get-tuple-element.43), custom_call_target="InvertDiagBlocksLowerTriangular" | custom-call | tf_op jit(solution)/shard_map/triangular_solve/custom-call.3 | solution.py:16
  523.4 11.9 %cholesky.534 = f32[128,128]{1,0:T(8,128)S(1)} custom-call(f32[128,128]{1,0:T(8,128)S(1)} %cholesky.759), custom_call_target="Cholesky" | custom-call | tf_op jit(solution)/shard_map/jit(cholesky)/cholesky | solution.py:14
  547.8 11.7 %cholesky.553 = f32[128,128]{1,0:T(8,128)S(1)} custom-call(f32[128,128]{1,0:T(8,128)S(1)} %cholesky.763), custom_call_target="Cholesky" | custom-call | tf_op jit(solution)/shard_map/jit(cholesky)/cholesky | solution.py:14
  572.3 12.1 %cholesky.574 = f32[128,128]{1,0:T(8,128)S(1)} custom-call(f32[128,128]{1,0:T(8,128)S(1)} %cholesky.768), custom_call_target="Cholesky" | custom-call | tf_op jit(solution)/shard_map/jit(cholesky)/cholesky | solution.py:14
  596.4 11.7 %cholesky.591 = f32[128,128]{1,0:T(8,128)S(1)} custom-call(f32[128,128]{1,0:T(8,128)S(1)} %convolution_subtract_fusion.24), custom_call_target="Cholesky" | custom-call | tf_op jit(solution)/shard_map/jit(cholesky)/cholesky | solution.py:14
  612.4 11.7 %while.11 = (s32[]{:T(128)}, f32[512,512]{1,0:T(8,128)}, s32[4,2]{0,1:T(2,128)S(1)}, f32[4,128,128]{2,1,0:T(8,128)S(1)}, s32[]{:T(128)}) while((s32[]{:T(128)}, f32[512,512]{1,0:T(8,128)}, s32[4,2]{0,1:T(2,128)S(1)}, f32[4,128,128]{2,1,0:T(8,128)S(1)}, s32[]{:T(128)}) %tuple.123), condition=%wide.while_cond.clone, body=%wide.while_body.clone.sunk | while | flops 2 | bytes 131181 | solution.py:16
  624.0 39.3 %custom-call.42 = f32[4,128,128]{1,2,0:T(8,128)S(1)} custom-call(f32[4,128,128]{2,1,0:T(8,128)S(1)} %get-tuple-element.44), custom_call_target="InvertDiagBlocksLowerTriangular" | custom-call | tf_op jit(solution)/shard_map/triangular_solve/custom-call.3 | solution.py:16
  672.0 28.8 %fusion.9 = f32[1024,1024]{1,0:T(8,128)S(1)} fusion(f32[2048,2048]{0,1:T(8,128)} %all-reduce.7.cloned.1.call-done, f32[512,512]{1,0:T(8,128)S(1)} %copy-done.9, f32[128,512]{1,0:T(8,128)S(1)} %fusion.126, f32[128,512]{1,0:T(8,128)S(1)} %fusion.127, f32[128,512]{1,0:T(8,128)S(1)} %fusion.129, f32[128,512]{1,0:T(8,128)S(1)} %fusion.82, ...), kind=kOutput, calls=%fused_computation.26 | convolution fusion | flops 12892241920 | bytes 11534336 | tf_op jit(solution)/shard_map/dot_general | solution.py:19
  700.9 16.8 %fusion.171 = f32[1024,1024]{1,0:T(8,128)} fusion(f32[1024,1024]{1,0:T(8,128)S(1)} %fusion.9, f32[512,512]{1,0:T(8,128)S(1)} %copy-done.9, f32[128,512]{1,0:T(8,128)S(1)} %fusion.126, f32[128,512]{1,0:T(8,128)S(1)} %fusion.127, f32[128,512]{1,0:T(8,128)S(1)} %fusion.129, f32[128,512]{1,0:T(8,128)S(1)} %fusion.82, f32[512,512]{1,0:T(8,128)S(1)} %convolution_negate_fusion.1), kind=kOutput, calls=%fused_computation.322 | convolution fusion | flops 12892241920 | bytes 11534336 | tf_op jit(solution)/shard_map/dot_general | solution.py:24
  717.7 15.8 %slice_subtract_fusion = f32[1024,1024]{0,1:T(8,128)S(1)} fusion(f32[2048,2048]{0,1:T(8,128)} %all-reduce.7.cloned.1.call-done, f32[1024,1024]{1,0:T(8,128)S(1)} %fusion.9), kind=kOutput, calls=%fused_computation.28 | convolution fusion | flops 12885950464 | bytes 16777216 | tf_op jit(solution)/shard_map/dot_general | solution.py:20
  740.4 11.7 %cholesky.606 = f32[128,128]{1,0:T(8,128)S(1)} custom-call(f32[128,128]{1,0:T(8,128)S(1)} %cholesky.772), custom_call_target="Cholesky" | custom-call | tf_op jit(solution)/shard_map/jit(cholesky)/cholesky | solution.py:14
  764.7 11.7 %cholesky.625 = f32[128,128]{1,0:T(8,128)S(1)} custom-call(f32[128,128]{1,0:T(8,128)S(1)} %cholesky.776), custom_call_target="Cholesky" | custom-call | tf_op jit(solution)/shard_map/jit(cholesky)/cholesky | solution.py:14
  789.5 11.7 %cholesky.646 = f32[128,128]{1,0:T(8,128)S(1)} custom-call(f32[128,128]{1,0:T(8,128)S(1)} %cholesky.781), custom_call_target="Cholesky" | custom-call | tf_op jit(solution)/shard_map/jit(cholesky)/cholesky | solution.py:14
  813.2 11.7 %cholesky.663 = f32[128,128]{1,0:T(8,128)S(1)} custom-call(f32[128,128]{1,0:T(8,128)S(1)} %convolution_subtract_fusion.23), custom_call_target="Cholesky" | custom-call | tf_op jit(solution)/shard_map/jit(cholesky)/cholesky | solution.py:14
  841.0 39.3 %custom-call.46 = f32[4,128,128]{1,2,0:T(8,128)S(1)} custom-call(f32[4,128,128]{2,1,0:T(8,128)S(1)} %get-tuple-element.45), custom_call_target="InvertDiagBlocksLowerTriangular" | custom-call | tf_op jit(solution)/shard_map/triangular_solve/custom-call.3 | solution.py:16
  907.0 11.7 %cholesky.678 = f32[128,128]{1,0:T(8,128)S(1)} custom-call(f32[128,128]{1,0:T(8,128)S(1)} %cholesky.785), custom_call_target="Cholesky" | custom-call | tf_op jit(solution)/shard_map/jit(cholesky)/cholesky | solution.py:14
  931.2 11.7 %cholesky.697 = f32[128,128]{1,0:T(8,128)S(1)} custom-call(f32[128,128]{1,0:T(8,128)S(1)} %cholesky.789), custom_call_target="Cholesky" | custom-call | tf_op jit(solution)/shard_map/jit(cholesky)/cholesky | solution.py:14
  955.8 11.7 %cholesky.718 = f32[128,128]{1,0:T(8,128)S(1)} custom-call(f32[128,128]{1,0:T(8,128)S(1)} %cholesky.794), custom_call_target="Cholesky" | custom-call | tf_op jit(solution)/shard_map/jit(cholesky)/cholesky | solution.py:14
  979.5 11.7 %cholesky.735 = f32[128,128]{1,0:T(8,128)S(1)} custom-call(f32[128,128]{1,0:T(8,128)S(1)} %convolution_subtract_fusion.22), custom_call_target="Cholesky" | custom-call | tf_op jit(solution)/shard_map/jit(cholesky)/cholesky | solution.py:14
  995.8 11.7 %while.13 = (s32[]{:T(128)}, f32[512,512]{1,0:T(8,128)}, s32[4,2]{0,1:T(2,128)S(1)}, f32[4,128,128]{2,1,0:T(8,128)S(1)}, s32[]{:T(128)}) while((s32[]{:T(128)}, f32[512,512]{1,0:T(8,128)}, s32[4,2]{0,1:T(2,128)S(1)}, f32[4,128,128]{2,1,0:T(8,128)S(1)}, s32[]{:T(128)}) %tuple.125), condition=%wide.while_cond.clone.2, body=%wide.while_body.clone.2.sunk | while | flops 2 | bytes 131181 | solution.py:16
  1007.5 39.3 %custom-call.50 = f32[4,128,128]{1,2,0:T(8,128)S(1)} custom-call(f32[4,128,128]{2,1,0:T(8,128)S(1)} %get-tuple-element.46), custom_call_target="InvertDiagBlocksLowerTriangular" | custom-call | tf_op jit(solution)/shard_map/triangular_solve/custom-call.3 | solution.py:16
  1060.6 13.6 %negate_convert_fusion = bf16[1024,1024]{1,0:T(8,128)(2,1)S(1)} fusion(f32[1024,1024]{1,0:T(8,128)S(1)} %copy-done.23, f32[512,512]{1,0:T(8,128)S(1)} %copy-done.11, f32[128,512]{1,0:T(8,128)S(1)} %fusion.114, f32[128,512]{1,0:T(8,128)S(1)} %fusion.115, f32[128,512]{1,0:T(8,128)S(1)} %fusion.117, f32[128,512]{1,0:T(8,128)S(1)} %fusion.78, ...), kind=kOutput, calls=%fused_computation.32 | convolution fusion | flops 12894339072 | bytes 9437184 | tf_op jit(solution)/shard_map/dot_general | solution.py:22
  1074.3 25.8 %fusion.15 = bf16[512,2048]{0,1:T(8,128)(2,1)S(1)} fusion(bf16[512,2048]{0,1:T(8,128)(2,1)S(1)} %copy-done.5, bf16[1024,1024]{1,0:T(8,128)(2,1)S(1)} %copy-done.19, bf16[1024,1024]{1,0:T(8,128)(2,1)S(1)} %fusion.18, bf16[1024,1024]{1,0:T(8,128)(2,1)S(1)} %negate_convert_fusion), kind=kOutput, calls=%fused_computation.34 | convolution fusion | flops 4329570304 | bytes 10485760 | tf_op jit(solution)/shard_map/dot_general | solution.py:76
  (304 shorter events, 329.4 us)
Async XLA Ops:
  6.5 8.1 copy-start
  6.5 4.7 copy-start.22
  6.5 6.8 copy-start.2
  6.5 7.4 copy-start.3
  6.5 8.7 copy-start.21
  6.5 31.0 %all-to-all-start = ((bf16[4,512,512]{2,1,0:T(8,128)(2,1)}), bf16[4,512,512]{2,1,0:T(8,128)(2,1)}, u32[]{:S(2)}, u32[]{:S(2)}) async-start(bf16[4,512,512]{2,1,0:T(8,128)(2,1)} %bitcast.231), calls=%async_computation | async-start | bytes 4194304 | tf_op jit(solution)/shard_map/all_to_all | solution.py:61
  11.1 360.1 %all-reduce.7.cloned.1.call-start = ((), (), s32[]{:S(2)}) async-start(), calls=%async_computation.1 | async-start | bytes 33554432 | tf_op jit(solution)/shard_map/psum | solution.py:74
  60.5 3.6 copy-start.4
  522.4 1.0 copy-start.14
  663.4 3.5 copy-start.20
  663.8 8.2 copy-start.9
  670.1 30.7 %copy-start.17 = (f32[128,512]{1,0:T(8,128)}, f32[128,512]{1,0:T(8,128)S(1)}, u32[]{:S(2)}) copy-start(f32[128,512]{1,0:T(8,128)S(1)} %fusion.126) | copy-start | bytes 786436
  672.0 28.9 %copy-start.6 = (f32[512,512]{1,0:T(8,128)}, f32[512,512]{1,0:T(8,128)S(1)}, u32[]{:S(2)}) copy-start(f32[512,512]{1,0:T(8,128)S(1)} %convolution_negate_fusion.1) | copy-start | bytes 3145732
  733.5 1.9 copy-start.12
  739.5 1.0 copy-start.16
  880.3 7.1 copy-start.13
  891.0 4.8 copy-start.7
  891.0 4.8 copy-start.10
  891.0 4.8 copy-start.18
  906.0 1.0 copy-start.15
  994.4 58.3 %copy-start.8 = (f32[512,512]{1,0:T(8,128)S(1)}, f32[512,512]{1,0:T(8,128)}, u32[]{:S(2)}) copy-start(f32[512,512]{1,0:T(8,128)} %fusion.169) | copy-start | bytes 3145732
  1047.2 7.4 copy-start.11
  1052.7 7.9 copy-start.23
  1060.6 13.7 %copy-start.5 = (bf16[512,2048]{0,1:T(8,128)(2,1)S(1)}, bf16[512,2048]{0,1:T(8,128)(2,1)}, u32[]{:S(2)}) copy-start(bf16[512,2048]{0,1:T(8,128)(2,1)} %copy-done.4) | copy-start | bytes 6291460
  1060.6 13.7 %copy-start.19 = (bf16[1024,1024]{1,0:T(8,128)(2,1)S(1)}, bf16[1024,1024]{1,0:T(8,128)(2,1)}, u32[]{:S(2)}) copy-start(bf16[1024,1024]{1,0:T(8,128)(2,1)} %fusion.172) | copy-start | bytes 6291460
  1074.3 28.2 %copy-start.1 = (bf16[64,8,128]{2,1,0:T(8,128)(2,1)S(1)}, bf16[64,8,128]{2,1,0:T(8,128)(2,1)}, u32[]{:S(2)}) copy-start(bf16[64,8,128]{2,1,0:T(8,128)(2,1)} %param.10) | copy-start | bytes 393220
Sparse Core Ops, SparseCore 0:
  91.8 279.3 all-reduce.6
where the time goes:
time: 1120 us; the launch traced here: 1110 us
  other arithmetic  502 us (45%)
  waiting for transfers between devices  301 us (27%)
  matrix products  194 us (17%)
  local copies, waits for them, and re-layouts  83.1 us (7%)
  between operations  25.2 us (2%)
    another operation x59, other arithmetic, inverse_factor(): lower = jnp.linalg.cholesky(matrix)  317 us
    psum x1, waiting for transfers between devices, shards(): metric = lax.psum(gram + paw, ('band', 'grid'))  279 us
    another operation x11, other arithmetic, inverse_factor(): lax.linalg.triangular_solve(lower, identity, left_side=True, lower=True)  163 us
    another operation x53, local copies, waits for them, and re-layouts, inverse_factor(): lax.linalg.triangular_solve(lower, identity, left_side=True, lower=True)  42.9 us
    dot_general x3, matrix products, inverse_factor(): jnp.dot(matrix[half:, :half], upper_inv.T, precision=lax.Precision.HIGHEST)  37.1 us
    dot_general x1, matrix products, shards(): jnp.dot(mine, inverse.T, preferred_element_type=jnp.float32)  25.8 us
  transfers between devices with their start and end apart: 2, of which 2 were waited for; matrix products, arithmetic and copies ran while one was open for 0% of the time, Pallas kernels for 0%

commit v1 on v0

--- a/solution.py
+++ b/solution.py
@@ -71,7 +71,7 @@
         correlations.reshape(-1, width_all),
         precision=lax.Precision.HIGHEST,
     )
-    metric = lax.psum(gram + paw, ("band", "grid"))
+    metric = lax.psum(lax.psum(gram + paw, "grid"), "band")
     inverse = inverse_factor(metric).astype(jnp.bfloat16)
     return jnp.dot(mine, inverse.T, preferred_element_type=jnp.float32).astype(jnp.bfloat16)
 

time: 1120 us -> 1640 us (1.46)
  waiting for transfers between devices: 301 us -> 822 us
    psum x1 -> x2, waiting for transfers between devices: 279 us -> 801 us  [shards(): metric = lax.psum(lax.psum(gram + paw, 'grid'), 'band')]
  transfers between devices with their start and end apart: 2 -> 3, of which waited for: 2 -> 3; matrix products, arithmetic and copies ran while one was open for 0% -> 0% of each run, Pallas kernels for 0% -> 0%
where the time goes in v1:
time: 1640 us; the launch traced here: 1630 us
  waiting for transfers between devices  822 us (50%)
  other arithmetic  502 us (31%)
  matrix products  194 us (12%)
  local copies, waits for them, and re-layouts  83.1 us (5%)
  between operations  25.2 us (2%)
    psum x2, waiting for transfers between devices, shards(): metric = lax.psum(lax.psum(gram + paw, 'grid'), 'band')  801 us
    another operation x59, other arithmetic, inverse_factor(): lower = jnp.linalg.cholesky(matrix)  317 us
    another operation x11, other arithmetic, inverse_factor(): lax.linalg.triangular_solve(lower, identity, left_side=True, lower=True)  163 us
    another operation x53, local copies, waits for them, and re-layouts, inverse_factor(): lax.linalg.triangular_solve(lower, identity, left_side=True, lower=True)  42.9 us
    dot_general x3, matrix products, inverse_factor(): jnp.dot(matrix[half:, :half], upper_inv.T, precision=lax.Precision.HIGHEST)  37.1 us
  transfers between devices with their start and end apart: 3, of which 3 were waited for; matrix products, arithmetic and copies ran while one was open for 0% of the time, Pallas kernels for 0%

profile of v1, /device:TPU:0, one launch (start us, length us, event | category | flops | bytes accessed | tf_op | source)
XLA Modules:
  0.0 1631.0 jit_solution(15490862944175929372)
XLA Ops:
  16.0 21.5 %all-to-all-done = bf16[4,512,512]{2,1,0:T(8,128)(2,1)} async-done(((bf16[4,512,512]{2,1,0:T(8,128)(2,1)}), bf16[4,512,512]{2,1,0:T(8,128)(2,1)}, u32[]{:S(2)}, u32[]{:S(2)}) %all-to-all-start) | async-done | bytes 2097184 | tf_op jit(solution)/shard_map/all_to_all | solution.py:61
  40.3 20.2 %while.9 = (s32[]{:T(128)}, bf16[512,2048]{0,1:T(8,128)(2,1)S(1)}, s32[8,2]{0,1:T(2,128)S(1)}, bf16[8,128,2048]{2,1,0:T(8,128)(2,1)}, s32[]{:T(128)}) while((s32[]{:T(128)}, bf16[512,2048]{0,1:T(8,128)(2,1)S(1)}, s32[8,2]{0,1:T(2,128)S(1)}, bf16[8,128,2048]{2,1,0:T(8,128)(2,1)}, s32[]{:T(128)}) %tuple.124), condition=%wide.while_cond.1, body=%wide.while_body.1.sunk | while | flops 2 | bytes 3146333 | solution.py:41
  64.7 14.1 fusion.178
  78.8 12.9 bitcast_add_fusion
  91.8 511.0 %all-reduce.8.cloned.1.call-done = f32[2048,2048]{0,1:T(8,128)} async-done(((f32[2048,2048]{0,1:T(8,128)}), f32[2048,2048]{0,1:T(8,128)}) %all-reduce.8.cloned.1.call-update) | async-done | bytes 16777232 | tf_op jit(solution)/shard_map/psum | solution.py:74
  602.9 289.7 %all-reduce.10.cloned.1.call-done = f32[2048,2048]{0,1:T(8,128)} async-done(((f32[2048,2048]{0,1:T(8,128)}), f32[2048,2048]{0,1:T(8,128)}) %all-reduce.10.cloned.1.call-update) | async-done | bytes 16777232 | tf_op jit(solution)/shard_map/psum | solution.py:74
  895.8 11.7 cholesky.462
  918.1 11.7 cholesky.481
  940.5 11.7 cholesky.502
  963.3 11.7 cholesky.519
  987.6 39.3 %custom-call.38 = f32[4,128,128]{1,2,0:T(8,128)S(1)} custom-call(f32[4,128,128]{2,1,0:T(8,128)S(1)} %get-tuple-element.43), custom_call_target="InvertDiagBlocksLowerTriangular" | custom-call | tf_op jit(solution)/shard_map/triangular_solve/custom-call.3 | solution.py:16
  1044.7 11.9 cholesky.534
  1069.0 11.7 cholesky.553
  1093.5 12.1 cholesky.574
  1117.6 11.7 cholesky.591
  1145.3 39.3 %custom-call.42 = f32[4,128,128]{1,2,0:T(8,128)S(1)} custom-call(f32[4,128,128]{2,1,0:T(8,128)S(1)} %get-tuple-element.44), custom_call_target="InvertDiagBlocksLowerTriangular" | custom-call | tf_op jit(solution)/shard_map/triangular_solve/custom-call.3 | solution.py:16
  1193.2 28.8 %fusion.9 = f32[1024,1024]{1,0:T(8,128)S(1)} fusion(f32[2048,2048]{0,1:T(8,128)} %all-reduce.10.cloned.1.call-done, f32[512,512]{1,0:T(8,128)S(1)} %copy-done.9, f32[128,512]{1,0:T(8,128)S(1)} %fusion.126, f32[128,512]{1,0:T(8,128)S(1)} %fusion.127, f32[128,512]{1,0:T(8,128)S(1)} %fusion.129, f32[128,512]{1,0:T(8,128)S(1)} %fusion.82, ...), kind=kOutput, calls=%fused_computation.26 | convolution fusion | flops 12892241920 | bytes 11534336 | tf_op jit(solution)/shard_map/dot_general | solution.py:19
  1222.1 16.8 %fusion.171 = f32[1024,1024]{1,0:T(8,128)} fusion(f32[1024,1024]{1,0:T(8,128)S(1)} %fusion.9, f32[512,512]{1,0:T(8,128)S(1)} %copy-done.9, f32[128,512]{1,0:T(8,128)S(1)} %fusion.126, f32[128,512]{1,0:T(8,128)S(1)} %fusion.127, f32[128,512]{1,0:T(8,128)S(1)} %fusion.129, f32[128,512]{1,0:T(8,128)S(1)} %fusion.82, f32[512,512]{1,0:T(8,128)S(1)} %convolution_negate_fusion.1), kind=kOutput, calls=%fused_computation.322 | convolution fusion | flops 12892241920 | bytes 11534336 | tf_op jit(solution)/shard_map/dot_general | solution.py:24
  1238.9 15.8 slice_subtract_fusion
  1261.7 11.7 cholesky.606
  1285.9 11.7 cholesky.625
  1310.8 11.7 cholesky.646
  1334.4 11.7 cholesky.663
  1362.2 39.3 %custom-call.46 = f32[4,128,128]{1,2,0:T(8,128)S(1)} custom-call(f32[4,128,128]{2,1,0:T(8,128)S(1)} %get-tuple-element.45), custom_call_target="InvertDiagBlocksLowerTriangular" | custom-call | tf_op jit(solution)/shard_map/triangular_solve/custom-call.3 | solution.py:16
  1428.2 11.7 cholesky.678
  1452.4 11.7 cholesky.697
  1477.0 11.7 cholesky.718
  1500.8 11.7 cholesky.735
  1517.0 11.7 while.13
  1528.7 39.3 %custom-call.50 = f32[4,128,128]{1,2,0:T(8,128)S(1)} custom-call(f32[4,128,128]{2,1,0:T(8,128)S(1)} %get-tuple-element.46), custom_call_target="InvertDiagBlocksLowerTriangular" | custom-call | tf_op jit(solution)/shard_map/triangular_solve/custom-call.3 | solution.py:16
  1581.8 13.6 negate_convert_fusion
  1595.5 25.8 %fusion.15 = bf16[512,2048]{0,1:T(8,128)(2,1)S(1)} fusion(bf16[512,2048]{0,1:T(8,128)(2,1)S(1)} %copy-done.5, bf16[1024,1024]{1,0:T(8,128)(2,1)S(1)} %copy-done.19, bf16[1024,1024]{1,0:T(8,128)(2,1)S(1)} %fusion.18, bf16[1024,1024]{1,0:T(8,128)(2,1)S(1)} %negate_convert_fusion), kind=kOutput, calls=%fused_computation.34 | convolution fusion | flops 4329570304 | bytes 10485760 | tf_op jit(solution)/shard_map/dot_general | solution.py:76
  (307 shorter events, 341.6 us)
Async XLA Ops:
  6.5 8.1 copy-start
  6.5 4.7 copy-start.22
  6.5 6.8 copy-start.2
  6.5 7.4 copy-start.3
  6.5 8.7 copy-start.21
  6.5 31.0 %all-to-all-start = ((bf16[4,512,512]{2,1,0:T(8,128)(2,1)}), bf16[4,512,512]{2,1,0:T(8,128)(2,1)}, u32[]{:S(2)}, u32[]{:S(2)}) async-start(bf16[4,512,512]{2,1,0:T(8,128)(2,1)} %bitcast.231), calls=%async_computation | async-start | bytes 4194304 | tf_op jit(solution)/shard_map/all_to_all | solution.py:61
  11.1 591.6 %all-reduce.8.cloned.1.call-start = ((), (), s32[]{:S(2)}) async-start(), calls=%async_computation.1 | async-start | bytes 33554432 | tf_op jit(solution)/shard_map/psum | solution.py:74
  60.5 3.6 copy-start.4
  91.7 800.9 %all-reduce.10.cloned.1.call-start = ((), (), s32[]{:S(2)}) async-start(), calls=%async_computation.2 | async-start | bytes 33554432 | tf_op jit(solution)/shard_map/psum | solution.py:74
  1043.6 1.0 copy-start.14
  1184.6 3.5 copy-start.20
  1185.0 8.2 copy-start.9
  1191.4 30.7 %copy-start.17 = (f32[128,512]{1,0:T(8,128)}, f32[128,512]{1,0:T(8,128)S(1)}, u32[]{:S(2)}) copy-start(f32[128,512]{1,0:T(8,128)S(1)} %fusion.126) | copy-start | bytes 786436
  1193.2 28.9 %copy-start.6 = (f32[512,512]{1,0:T(8,128)}, f32[512,512]{1,0:T(8,128)S(1)}, u32[]{:S(2)}) copy-start(f32[512,512]{1,0:T(8,128)S(1)} %convolution_negate_fusion.1) | copy-start | bytes 3145732
  1254.7 1.9 copy-start.12
  1260.7 1.0 copy-start.16
  1401.6 7.1 copy-start.13
  1412.2 4.8 copy-start.7
  1412.2 4.8 copy-start.10
  1412.3 4.8 copy-start.18
  1427.2 1.0 copy-start.15
  1515.6 58.3 %copy-start.8 = (f32[512,512]{1,0:T(8,128)S(1)}, f32[512,512]{1,0:T(8,128)}, u32[]{:S(2)}) copy-start(f32[512,512]{1,0:T(8,128)} %fusion.169) | copy-start | bytes 3145732
  1568.4 7.4 copy-start.11
  1574.0 7.9 copy-start.23
  1581.8 13.7 copy-start.5
  1581.8 13.7 copy-start.19
  1595.5 28.2 %copy-start.1 = (bf16[64,8,128]{2,1,0:T(8,128)(2,1)S(1)}, bf16[64,8,128]{2,1,0:T(8,128)(2,1)}, u32[]{:S(2)}) copy-start(bf16[64,8,128]{2,1,0:T(8,128)(2,1)} %param.10) | copy-start | bytes 393220
Sparse Core Ops, SparseCore 0:
  91.8 510.8 all-reduce.7
  605.3 287.3 all-reduce.9
